TPU v7x, 1024 devices: a whole 4x4x32 slice. The times are simulated.
1024 devices in a mesh: ep: 16 (over x_hi, y, core), dp: 64 (over x_lo, z).
Axes of the slice: x: 4 (x_hi: 2, x_lo: 2; x = x_hi * 2 + x_lo), y: 4, z: 32, core: 2. Of those that a mesh axis runs over, the one named last changes fastest.
Arguments:
- fwd_tokens: bfloat16 [16384, 2048], P(('ep', 'dp')), may hold values from -6 to 6
- fwd_routes: int32 [16384, 8], P(('ep', 'dp')), may hold values from 0 to 15, as said below
- fwd_weights: float32 [16384, 8], P(('ep', 'dp')), may hold values from 0.05 to 0.4
- bwd_grads: bfloat16 [16384, 2048], P(('ep', 'dp')), may hold values from -24 to 24
- bwd_routes: int32 [16384, 8], P(('ep', 'dp')), may hold values from 0 to 15, as said below
- bwd_weights: float32 [16384, 8], P(('ep', 'dp')), may hold values from 0.05 to 0.4
- bwd_saved: bfloat16 [16, 8192, 2048], P('ep', 'dp'), may hold values from -6 to 6
- w_gate: bfloat16 [16, 2048, 384], P('ep'), may hold values from -0.125 to 0.125
- w_up: bfloat16 [16, 2048, 384], P('ep'), may hold values from -0.125 to 0.125
- w_down: bfloat16 [16, 384, 2048], P('ep'), may hold values from -0.3125 to 0.3125
Outputs:
- fwd_out: bfloat16 [16384, 2048], P(('ep', 'dp'))
- bwd_input_grad: bfloat16 [16384, 2048], P(('ep', 'dp'))
- down_grad: float32 [16, 2048, 384], P('ep', 'dp')
Inputs may be any that keep to these rules, and one draw needn't show every extreme that they name: `fwd_routes`: each token names 8 different experts, and the 16 tokens of each aligned block (one device's tokens) name every expert exactly 8 times. `bwd_routes`: each token names 8 different experts, and the 16 tokens of each aligned block (one device's tokens) name every expert exactly 8 times.
All inputs are finite; a program needn't handle non-finite values.
Results may differ from a plain program's by a relative error of at most 0.0064.
Values may be sent and summed in bfloat16 or wider, within the bound.
No kernel may reach another device: no remote copies, remote signals or barrier semaphores. Data moves between devices by JAX's collectives and lax.ppermute only.
A program may use at most 32 MiB of HBM per device.

v0:
```python
import jax
import jax.numpy as jnp
from jax import lax
from jax.experimental import pallas as pl
from jax.sharding import PartitionSpec as P

EXPERTS = 16
SLOTS = 8
NEAR = 4
BF16, F32 = jnp.bfloat16, jnp.float32


def slot_matrix(routes_t, weights_t):
    picks, tokens = routes_t.shape
    rows = EXPERTS * SLOTS
    row = lax.broadcasted_iota(jnp.int32, (rows, tokens), 0)
    expert, slot = row // SLOTS, row % SLOTS
    member = jnp.zeros((rows, tokens), F32)
    mixing = jnp.zeros((rows, tokens), F32)
    for k in range(picks):
        hit = routes_t[k : k + 1, :] == expert
        member = member + jnp.where(hit, 1.0, 0.0)
        mixing = mixing + jnp.where(hit, weights_t[k : k + 1, :], 0.0)
    earlier = lax.broadcasted_iota(jnp.int32, (tokens, tokens), 0) < lax.broadcasted_iota(
        jnp.int32, (tokens, tokens), 1
    )
    before = jnp.dot(
        member.astype(BF16), jnp.where(earlier, 1.0, 0.0).astype(BF16), preferred_element_type=F32
    )
    chosen = (member > 0.5) & (before.astype(jnp.int32) == slot)
    return jnp.where(chosen, 1.0, 0.0), jnp.where(chosen, mixing, 0.0)


def select_kernel(scaled, routes_ref, weights_ref, x_ref, out_ref):
    chosen, mixing = slot_matrix(routes_ref[...], weights_ref[...])
    scale = jnp.sum(mixing, axis=1, keepdims=True)
    chosen = chosen.astype(BF16)
    for c in range(0, x_ref.shape[1], 256):
        rows = jnp.dot(chosen, x_ref[:, c : c + 256], preferred_element_type=F32)
        if scaled:
            rows = rows * scale
        out_ref[:, c : c + 256] = rows.astype(BF16)


def select(routes, weights, x, scaled):
    import functools

    rows, width = EXPERTS * SLOTS, x.shape[1]
    return pl.pallas_call(
        functools.partial(select_kernel, scaled),
        out_shape=jax.ShapeDtypeStruct((rows, width), BF16),
        cost_estimate=pl.CostEstimate(flops=2 * rows * 16 * width, bytes_accessed=rows * width * 4, transcendentals=0),
        name="select_scaled" if scaled else "select_plain",
    )(routes.T, weights.T, x)


def combine_kernel(weighted, routes_ref, weights_ref, rows_ref, out_ref):
    chosen, mixing = slot_matrix(routes_ref[...], weights_ref[...])
    if weighted:
        high = mixing.astype(BF16)
        rest = mixing - high.astype(F32)
        middle = rest.astype(BF16)
        low = (rest - middle.astype(F32)).astype(BF16)
        parts = [low, middle, high]
    else:
        parts = [chosen.astype(BF16)]
    parts = [p.astype(F32).T.astype(BF16) for p in parts]
    for c in range(0, rows_ref.shape[1], 512):
        rows = rows_ref[:, c : c + 512]
        total = jnp.dot(parts[0], rows, preferred_element_type=F32)
        for p in parts[1:]:
            total = total + jnp.dot(p, rows, preferred_element_type=F32)
        out_ref[:, c : c + 512] = total.astype(BF16)


def combine(routes, weights, rows, weighted):
    import functools

    return pl.pallas_call(
        functools.partial(combine_kernel, weighted),
        out_shape=jax.ShapeDtypeStruct((routes.shape[0], rows.shape[1]), BF16),
        cost_estimate=pl.CostEstimate(flops=10**7, bytes_accessed=rows.size * 2, transcendentals=0),
        name="combine_weighted" if weighted else "combine_plain",
    )(routes.T, weights.T, rows)


def on_device(
    fwd_tokens, fwd_routes, fwd_weights, bwd_grads, bwd_routes, bwd_weights, bwd_saved, w_gate, w_up, w_down
):
    dp = lax.axis_size("dp")
    depth = dp // 2
    me = lax.axis_index("dp")
    upper = lax.shift_right_logical(me, depth.bit_length() - 1) & 1
    width = fwd_tokens.shape[1]
    rows = EXPERTS * SLOTS
    contract_last = (((1,), (1,)), ((), ()))
    contract_rows = (((0,), (0,)), ((), ()))
    gate_w, up_w, down_w = w_gate[0], w_up[0], w_down[0]

    def all_swap(x, axis, groups=None):
        return lax.all_to_all(x, axis, split_axis=0, concat_axis=0, tiled=True, axis_index_groups=groups)

    def exchange(x):
        return all_swap(x.reshape(EXPERTS, SLOTS, width), "ep").reshape(rows, width)

    def piece(x, index, size, axis):
        start = [0] * x.ndim
        start[axis] = index * size
        shape = x.shape[:axis] + (size,) + x.shape[axis + 1 :]
        return lax.dynamic_slice(x, start, shape, allow_negative_indices=False)

    def with_partner(x, bit):
        return lax.ppermute(x, "dp", [(d, d ^ bit) for d in range(dp)])

    cot = exchange(select(bwd_routes, bwd_weights, bwd_grads, True))
    rows_a = exchange(select(fwd_routes, fwd_weights, fwd_tokens, False))

    gate_b = jnp.dot(bwd_saved[0], gate_w, preferred_element_type=F32)
    up_b = jnp.dot(bwd_saved[0], up_w, preferred_element_type=F32)
    sig = jax.nn.sigmoid(gate_b)
    act_b = (gate_b * sig * up_b).astype(BF16)
    act_far = with_partner(act_b, depth)

    half = width // 2
    cot_far = with_partner(piece(cot, 1 - upper, half, 1), depth)
    cot_near = piece(cot, upper, half, 1)
    total = lax.dot_general(cot_near, act_b, contract_rows, preferred_element_type=F32)
    total = total + lax.dot_general(cot_far, act_far, contract_rows, preferred_element_type=F32)

    count, bit = depth, 1
    block = half // depth
    total = total.reshape(count, block, total.shape[1])
    while bit < NEAR:
        mine = lax.shift_right_logical(me, bit.bit_length() - 1) & 1
        pairs = total.reshape(count // 2, 2, block, total.shape[2])
        away = piece(pairs, 1 - mine, 1, 1).squeeze(1).astype(BF16)
        kept = piece(pairs, mine, 1, 1).squeeze(1)
        total = kept + with_partner(away, bit).astype(F32)
        count, bit = count // 2, bit * 2
    groups = [[x * depth + f * NEAR + k for f in range(count)] for x in range(2) for k in range(NEAR)]
    parts = all_swap(total.astype(BF16), "dp", groups)
    down_grad = jnp.sum(parts.astype(F32), axis=0)[None]

    dact = lax.dot_general(cot, down_w, contract_last, preferred_element_type=F32)
    dgate = (dact * up_b * sig * (1.0 + gate_b * (1.0 - sig))).astype(BF16)
    dup = (dact * gate_b * sig).astype(BF16)
    row_b = lax.dot_general(dgate, gate_w, contract_last, preferred_element_type=F32)
    row_b = row_b + lax.dot_general(dup, up_w, contract_last, preferred_element_type=F32)
    back_b = exchange(row_b.astype(BF16))

    gate_a = jnp.dot(rows_a, gate_w, preferred_element_type=F32)
    up_a = jnp.dot(rows_a, up_w, preferred_element_type=F32)
    act_a = (jax.nn.silu(gate_a) * up_a).astype(BF16)
    row_a = jnp.dot(act_a, down_w, preferred_element_type=F32).astype(BF16)
    back_a = exchange(row_a)

    fwd_out = combine(fwd_routes, fwd_weights, back_a, True)
    input_grad = combine(bwd_routes, bwd_weights, back_b, False)
    return fwd_out, input_grad, down_grad


def solution(mesh):
    in_specs = (P(("ep", "dp"), None),) * 6 + (P("ep", "dp", None),) + (P("ep", None, None),) * 3
    out_specs = (P(("ep", "dp"), None), P(("ep", "dp"), None), P("ep", "dp", None))

    return jax.shard_map(on_device, mesh=mesh, in_specs=in_specs, out_specs=out_specs, check_vma=False)
```

profile of v0, /device:TPU:4, one launch (start us, length us, event | category | flops | bytes accessed | tf_op | source)
XLA Modules:
  0.0 156.0 jit_solution(9745336025703740703)
XLA Ops:
  0.7 2.3 %select_plain.1 = bf16[128,2048]{1,0:T(8,128)(2,1)} custom-call(s32[8,16]{1,0:T(8,128)} %bitcast.79, f32[8,16]{1,0:T(8,128)} %bitcast.81, bf16[16,2048]{1,0:T(8,128)(2,1)} %x_ref.2), custom_call_target="tpu_custom_call" | custom-call | flops 8388608 | bytes 1048576 | tf_op jit(solution)/shard_map/select_plain/pallas_call | solution.py:49
  2.9 17.1 %all-to-all-start = ((bf16[16,8,2048]{2,1,0:T(8,128)(2,1)}), bf16[16,8,2048]{2,1,0:T(8,128)(2,1)}, u32[]{:S(2)}, u32[]{:S(2)}) async-start(bf16[16,8,2048]{2,1,0:T(8,128)(2,1)} %bitcast.75), calls=%async_computation | async-start | bytes 1048576 | tf_op jit(solution)/shard_map/all_to_all | solution.py:101
  20.1 1.5 fusion.13
  21.6 1.2 multiply_convert_fusion
  22.8 1.9 %collective-permute-start.1 = (bf16[128,384]{1,0:T(8,128)(2,1)}, bf16[128,384]{1,0:T(8,128)(2,1)}, u32[]{:S(2)}, u32[]{:S(2)}) collective-permute-start(bf16[128,384]{1,0:T(8,128)(2,1)} %get-tuple-element.3), channel_id=1, source_target_pairs={{0,32},{1,33},{2,34},{3,35},{4,36},{5,37},{6,38},{7,39},{8,40},{9,... | collective-permute-start | bytes 294920 | tf_op jit(solution)/shard_map/ppermute | solution.py:113
  24.7 2.1 %select_scaled.1 = bf16[128,2048]{1,0:T(8,128)(2,1)} custom-call(s32[8,16]{1,0:T(8,128)} %bitcast.83, f32[8,16]{1,0:T(8,128)} %bitcast.85, bf16[16,2048]{1,0:T(8,128)(2,1)} %x_ref.3), custom_call_target="tpu_custom_call" | custom-call | flops 8388608 | bytes 1048576 | tf_op jit(solution)/shard_map/select_scaled/pallas_call | solution.py:49
  26.9 3.3 %all-to-all-done = bf16[16,8,2048]{2,1,0:T(8,128)(2,1)} async-done(((bf16[16,8,2048]{2,1,0:T(8,128)(2,1)}), bf16[16,8,2048]{2,1,0:T(8,128)(2,1)}, u32[]{:S(2)}, u32[]{:S(2)}) %all-to-all-start) | async-done | bytes 524320 | tf_op jit(solution)/shard_map/all_to_all | solution.py:101
  30.2 7.0 %all-to-all-start.2 = ((bf16[16,8,2048]{2,1,0:T(8,128)(2,1)}), bf16[16,8,2048]{2,1,0:T(8,128)(2,1)}, u32[]{:S(2)}, u32[]{:S(2)}) async-start(bf16[16,8,2048]{2,1,0:T(8,128)(2,1)} %bitcast.77), calls=%async_computation.2 | async-start | bytes 1048576 | tf_op jit(solution)/shard_map/all_to_all | solution.py:101
  37.2 1.5 fusion.15
  38.7 3.2 %fusion.1 = bf16[16,8,2048]{2,1,0:T(8,128)(2,1)} fusion(bf16[1,384,2048]{2,1,0:T(8,128)(2,1)} %param.19, bf16[1,2048,384]{2,1,0:T(8,128)(2,1)S(1)} %copy-done, bf16[16,8,2048]{2,1,0:T(8,128)(2,1)} %all-to-all-done, f32[128,384]{1,0:T(8,128)S(1)} %fusion.15), kind=kOutput, calls=%fused_computation.3 | convolution fusion | flops 403210240 | bytes 4390912 | tf_op jit(solution)/shard_map/dot_general | solution.py:154
  41.9 4.9 %all-to-all-done.2 = bf16[16,8,2048]{2,1,0:T(8,128)(2,1)} async-done(((bf16[16,8,2048]{2,1,0:T(8,128)(2,1)}), bf16[16,8,2048]{2,1,0:T(8,128)(2,1)}, u32[]{:S(2)}, u32[]{:S(2)}) %all-to-all-start.2) | async-done | bytes 524320 | tf_op jit(solution)/shard_map/all_to_all | solution.py:101
  46.8 7.0 %all-to-all-start.1 = ((bf16[16,8,2048]{2,1,0:T(8,128)(2,1)}), bf16[16,8,2048]{2,1,0:T(8,128)(2,1)}, u32[]{:S(2)}, u32[]{:S(2)}) async-start(bf16[16,8,2048]{2,1,0:T(8,128)(2,1)} %fusion.1), calls=%async_computation.1 | async-start | bytes 1048576 | tf_op jit(solution)/shard_map/all_to_all | solution.py:101
  53.8 1.0 constant_dynamic-slice_fusion
  54.8 1.9 %collective-permute-start = (bf16[128,1024]{1,0:T(8,128)(2,1)S(1)}, bf16[128,1024]{1,0:T(8,128)(2,1)S(1)}, u32[]{:S(2)}, u32[]{:S(2)}) collective-permute-start(bf16[128,1024]{1,0:T(8,128)(2,1)S(1)} %constant_dynamic-slice_fusion), channel_id=1, source_target_pairs={{0,32},{1,33},{2,34},{3,35},{4,36},{5,37},{6,38},{7,39},{8,40},{9,... | collective-permute-start | bytes 786440 | tf_op jit(solution)/shard_map/ppermute | solution.py:113
  56.7 2.2 %fusion.3 = f32[128,384]{1,0:T(8,128)S(1)} fusion(bf16[1,384,2048]{2,1,0:T(8,128)(2,1)} %param.19, bf16[16,8,2048]{2,1,0:T(8,128)(2,1)} %all-to-all-done.2), kind=kOutput, calls=%fused_computation.5 | convolution fusion | flops 201326592 | bytes 2293760 | tf_op jit(solution)/shard_map/dot_general | solution.py:144
  58.9 1.4 fusion.32
  60.3 5.5 %collective-permute-done = bf16[128,1024]{1,0:T(8,128)(2,1)S(1)} collective-permute-done((bf16[128,1024]{1,0:T(8,128)(2,1)S(1)}, bf16[128,1024]{1,0:T(8,128)(2,1)S(1)}, u32[]{:S(2)}, u32[]{:S(2)}) %collective-permute-start) | collective-permute-done | bytes 262176 | tf_op jit(solution)/shard_map/ppermute | solution.py:113
  65.7 1.3 convolution_add_fusion.1
  67.1 1.9 %collective-permute-start.2 = (bf16[16,32,384]{2,1,0:T(8,128)(2,1)S(1)}, bf16[16,32,384]{2,1,0:T(8,128)(2,1)S(1)}, u32[]{:S(2)}, u32[]{:S(2)}) collective-permute-start(bf16[16,32,384]{2,1,0:T(8,128)(2,1)S(1)} %fusion.30), channel_id=1, source_target_pairs={{0,1},{1,0},{2,3},{3,2},{4,5},{5,4},{6,7},{7,6},{8,9},{9,8},{10,11... | collective-permute-start | bytes 1179656 | tf_op jit(solution)/shard_map/ppermute | solution.py:113
  69.0 0.6 fusion.11
  69.7 1.5 fusion.2
  71.1 8.4 %collective-permute-done.2 = bf16[16,32,384]{2,1,0:T(8,128)(2,1)S(1)} collective-permute-done((bf16[16,32,384]{2,1,0:T(8,128)(2,1)S(1)}, bf16[16,32,384]{2,1,0:T(8,128)(2,1)S(1)}, u32[]{:S(2)}, u32[]{:S(2)}) %collective-permute-start.2) | collective-permute-done | bytes 393248 | tf_op jit(solution)/shard_map/ppermute | solution.py:113
  79.6 0.1 bitcast_add_fusion
  79.7 7.3 %all-to-all-start.3 = ((bf16[16,8,2048]{2,1,0:T(8,128)(2,1)}), bf16[16,8,2048]{2,1,0:T(8,128)(2,1)S(1)}, u32[]{:S(2)}, u32[]{:S(2)}) async-start(bf16[16,8,2048]{2,1,0:T(8,128)(2,1)} %fusion.2), calls=%async_computation.3 | async-start | bytes 1048576 | tf_op jit(solution)/shard_map/all_to_all | solution.py:101
  87.0 1.9 %collective-permute-start.3 = (bf16[8,32,384]{2,1,0:T(8,128)(2,1)S(1)}, bf16[8,32,384]{2,1,0:T(8,128)(2,1)S(1)}, u32[]{:S(2)}, u32[]{:S(2)}) collective-permute-start(bf16[8,32,384]{2,1,0:T(8,128)(2,1)S(1)} %fusion.34), channel_id=1, source_target_pairs={{0,2},{1,3},{2,0},{3,1},{4,6},{5,7},{6,4},{7,5},{8,10},{9,11},{10,... | collective-permute-start | bytes 589832 | tf_op jit(solution)/shard_map/ppermute | solution.py:113
  88.9 11.7 %collective-permute-done.3 = bf16[8,32,384]{2,1,0:T(8,128)(2,1)S(1)} collective-permute-done((bf16[8,32,384]{2,1,0:T(8,128)(2,1)S(1)}, bf16[8,32,384]{2,1,0:T(8,128)(2,1)S(1)}, u32[]{:S(2)}, u32[]{:S(2)}) %collective-permute-start.3) | collective-permute-done | bytes 196640 | tf_op jit(solution)/shard_map/ppermute | solution.py:113
  100.6 0.7 fusion.31
  101.3 20.4 %all-to-all-start.4 = ((bf16[8,32,384]{2,1,0:T(8,128)(2,1)}), bf16[8,32,384]{2,1,0:T(8,128)(2,1)S(1)}, u32[]{:S(2)}, u32[]{:S(2)}) async-start(bf16[8,32,384]{2,1,0:T(8,128)(2,1)} %fusion.31), calls=%async_computation.4 | async-start | bytes 393216 | tf_op jit(solution)/shard_map/all_to_all | solution.py:101
  121.7 2.2 %combine_weighted.1 = bf16[16,2048]{1,0:T(8,128)(2,1)} custom-call(s32[8,16]{1,0:T(8,128)} %bitcast.80, f32[8,16]{1,0:T(8,128)} %bitcast.82, bf16[128,2048]{1,0:T(8,128)(2,1)} %bitcast.8.rows_ref), custom_call_target="tpu_custom_call" | custom-call | flops 10000000 | bytes 524288 | tf_op jit(solution)/shard_map/combine_weighted/pallas_call | solution.py:79
  124.0 2.1 %combine_plain.1 = bf16[16,2048]{1,0:T(8,128)(2,1)} custom-call(s32[8,16]{1,0:T(8,128)} %bitcast.84, f32[8,16]{1,0:T(8,128)} %bitcast.86, bf16[128,2048]{1,0:T(8,128)(2,1)} %bitcast.76), custom_call_target="tpu_custom_call" | custom-call | flops 10000000 | bytes 524288 | tf_op jit(solution)/shard_map/combine_plain/pallas_call | solution.py:79
  126.1 29.3 %all-to-all-done.4 = bf16[8,32,384]{2,1,0:T(8,128)(2,1)S(1)} async-done(((bf16[8,32,384]{2,1,0:T(8,128)(2,1)}), bf16[8,32,384]{2,1,0:T(8,128)(2,1)S(1)}, u32[]{:S(2)}, u32[]{:S(2)}) %all-to-all-start.4) | async-done | bytes 196640 | tf_op jit(solution)/shard_map/all_to_all | solution.py:101
  155.4 0.6 convert_reduce_fusion
  (15 shorter events, 0.1 us)
Async XLA Ops:
  0.6 21.0 %copy-start = (bf16[1,2048,384]{2,1,0:T(8,128)(2,1)S(1)}, bf16[1,2048,384]{2,1,0:T(8,128)(2,1)}, u32[]{:S(2)}) copy-start(bf16[1,2048,384]{2,1,0:T(8,128)(2,1)} %param.18) | copy-start | bytes 4718596
  0.6 19.4 %copy-start.1 = (bf16[1,2048,384]{2,1,0:T(8,128)(2,1)S(1)}, bf16[1,2048,384]{2,1,0:T(8,128)(2,1)}, u32[]{:S(2)}) copy-start(bf16[1,2048,384]{2,1,0:T(8,128)(2,1)} %param.17) | copy-start | bytes 4718596
  2.9 27.3 %all-to-all-start = ((bf16[16,8,2048]{2,1,0:T(8,128)(2,1)}), bf16[16,8,2048]{2,1,0:T(8,128)(2,1)}, u32[]{:S(2)}, u32[]{:S(2)}) async-start(bf16[16,8,2048]{2,1,0:T(8,128)(2,1)} %bitcast.75), calls=%async_computation | async-start | bytes 1048576 | tf_op jit(solution)/shard_map/all_to_all | solution.py:101
  20.1 1.6 %copy-start.3 = (bf16[1,128,2048]{2,1,0:T(8,128)(2,1)S(1)}, bf16[1,128,2048]{2,1,0:T(8,128)(2,1)}, u32[]{:S(2)}) copy-start(bf16[1,128,2048]{2,1,0:T(8,128)(2,1)} %param.16) | copy-start | bytes 1572868
  22.8 37.4 %collective-permute-start.1 = (bf16[128,384]{1,0:T(8,128)(2,1)}, bf16[128,384]{1,0:T(8,128)(2,1)}, u32[]{:S(2)}, u32[]{:S(2)}) collective-permute-start(bf16[128,384]{1,0:T(8,128)(2,1)} %get-tuple-element.3), channel_id=1, source_target_pairs={{0,32},{1,33},{2,34},{3,35},{4,36},{5,37},{6,38},{7,39},{8,40},{9,... | collective-permute-start | bytes 294920 | tf_op jit(solution)/shard_map/ppermute | solution.py:113
  30.2 16.6 %all-to-all-start.2 = ((bf16[16,8,2048]{2,1,0:T(8,128)(2,1)}), bf16[16,8,2048]{2,1,0:T(8,128)(2,1)}, u32[]{:S(2)}, u32[]{:S(2)}) async-start(bf16[16,8,2048]{2,1,0:T(8,128)(2,1)} %bitcast.77), calls=%async_computation.2 | async-start | bytes 1048576 | tf_op jit(solution)/shard_map/all_to_all | solution.py:101
  46.8 32.9 %all-to-all-start.1 = ((bf16[16,8,2048]{2,1,0:T(8,128)(2,1)}), bf16[16,8,2048]{2,1,0:T(8,128)(2,1)}, u32[]{:S(2)}, u32[]{:S(2)}) async-start(bf16[16,8,2048]{2,1,0:T(8,128)(2,1)} %fusion.1), calls=%async_computation.1 | async-start | bytes 1048576 | tf_op jit(solution)/shard_map/all_to_all | solution.py:101
  54.8 11.0 %collective-permute-start = (bf16[128,1024]{1,0:T(8,128)(2,1)S(1)}, bf16[128,1024]{1,0:T(8,128)(2,1)S(1)}, u32[]{:S(2)}, u32[]{:S(2)}) collective-permute-start(bf16[128,1024]{1,0:T(8,128)(2,1)S(1)} %constant_dynamic-slice_fusion), channel_id=1, source_target_pairs={{0,32},{1,33},{2,34},{3,35},{4,36},{5,37},{6,38},{7,39},{8,40},{9,... | collective-permute-start | bytes 786440 | tf_op jit(solution)/shard_map/ppermute | solution.py:113
  60.2 8.8 %copy-start.4 = (f32[128,384]{1,0:T(8,128)S(1)}, f32[128,384]{1,0:T(8,128)}, u32[]{:S(2)}) copy-start(f32[128,384]{1,0:T(8,128)} %get-tuple-element.4) | copy-start | bytes 589828
  67.1 12.5 %collective-permute-start.2 = (bf16[16,32,384]{2,1,0:T(8,128)(2,1)S(1)}, bf16[16,32,384]{2,1,0:T(8,128)(2,1)S(1)}, u32[]{:S(2)}, u32[]{:S(2)}) collective-permute-start(bf16[16,32,384]{2,1,0:T(8,128)(2,1)S(1)} %fusion.30), channel_id=1, source_target_pairs={{0,1},{1,0},{2,3},{3,2},{4,5},{5,4},{6,7},{7,6},{8,9},{9,8},{10,11... | collective-permute-start | bytes 1179656 | tf_op jit(solution)/shard_map/ppermute | solution.py:113
  79.7 21.7 %all-to-all-start.3 = ((bf16[16,8,2048]{2,1,0:T(8,128)(2,1)}), bf16[16,8,2048]{2,1,0:T(8,128)(2,1)S(1)}, u32[]{:S(2)}, u32[]{:S(2)}) async-start(bf16[16,8,2048]{2,1,0:T(8,128)(2,1)} %fusion.2), calls=%async_computation.3 | async-start | bytes 1048576 | tf_op jit(solution)/shard_map/all_to_all | solution.py:101
  87.0 13.7 %collective-permute-start.3 = (bf16[8,32,384]{2,1,0:T(8,128)(2,1)S(1)}, bf16[8,32,384]{2,1,0:T(8,128)(2,1)S(1)}, u32[]{:S(2)}, u32[]{:S(2)}) collective-permute-start(bf16[8,32,384]{2,1,0:T(8,128)(2,1)S(1)} %fusion.34), channel_id=1, source_target_pairs={{0,2},{1,3},{2,0},{3,1},{4,6},{5,7},{6,4},{7,5},{8,10},{9,11},{10,... | collective-permute-start | bytes 589832 | tf_op jit(solution)/shard_map/ppermute | solution.py:113
  101.3 22.6 %copy-start.2 = (bf16[16,8,2048]{2,1,0:T(8,128)(2,1)}, bf16[16,8,2048]{2,1,0:T(8,128)(2,1)S(1)}, u32[]{:S(2)}) copy-start(bf16[16,8,2048]{2,1,0:T(8,128)(2,1)S(1)} %all-to-all-done.3) | copy-start | bytes 1572868
  101.3 54.0 %all-to-all-start.4 = ((bf16[8,32,384]{2,1,0:T(8,128)(2,1)}), bf16[8,32,384]{2,1,0:T(8,128)(2,1)S(1)}, u32[]{:S(2)}, u32[]{:S(2)}) async-start(bf16[8,32,384]{2,1,0:T(8,128)(2,1)} %fusion.31), calls=%async_computation.4 | async-start | bytes 393216 | tf_op jit(solution)/shard_map/all_to_all | solution.py:101
where the time goes:
time: 157 us; the launch traced here: 156 us
  starting transfers between devices  66.5 us (42%)
  waiting for transfers between devices  63.1 us (40%)
  matrix products  14.3 us (9%)
  Pallas kernels  8.72 us (6%)
    all_to_all x5, starting transfers between devices, all_swap(): lax.all_to_all(x, axis, split_axis=0, concat_axis=0, tiled=True, axis_ind...  58.9 us
    all_to_all x5, waiting for transfers between devices, all_swap(): lax.all_to_all(x, axis, split_axis=0, concat_axis=0, tiled=True, axis_ind...  37.5 us
    ppermute x4, waiting for transfers between devices, with_partner(): return lax.ppermute(x, 'dp', [(d, d ^ bit) for d in range(dp)])  25.6 us
    ppermute x4, starting transfers between devices, with_partner(): return lax.ppermute(x, 'dp', [(d, d ^ bit) for d in range(dp)])  7.67 us
    pallas_call x2, Pallas kernels, select(): pl.pallas_call(functools.partial(select_kernel, scaled), out_shape=jax.Sh...  4.38 us
    pallas_call x2, Pallas kernels, combine(): pl.pallas_call(functools.partial(combine_kernel, weighted), out_shape=jax...  4.34 us
    dot_general x1, matrix products, on_device(): row_a = jnp.dot(act_a, down_w, preferred_element_type=F32).astype(BF16)  3.22 us
  transfers between devices with their start and end apart: 9, of which 6 were waited for; matrix products, arithmetic and copies ran while one was open for 10% of the time, Pallas kernels for 4%

commit v1 on v0

--- a/solution.py
+++ b/solution.py
@@ -6,7 +6,6 @@
 
 EXPERTS = 16
 SLOTS = 8
-NEAR = 4
 BF16, F32 = jnp.bfloat16, jnp.float32
 
 
@@ -97,11 +96,9 @@
     contract_rows = (((0,), (0,)), ((), ()))
     gate_w, up_w, down_w = w_gate[0], w_up[0], w_down[0]
 
-    def all_swap(x, axis, groups=None):
-        return lax.all_to_all(x, axis, split_axis=0, concat_axis=0, tiled=True, axis_index_groups=groups)
-
     def exchange(x):
-        return all_swap(x.reshape(EXPERTS, SLOTS, width), "ep").reshape(rows, width)
+        x = x.reshape(EXPERTS, SLOTS, width)
+        return lax.all_to_all(x, "ep", split_axis=0, concat_axis=0, tiled=True).reshape(rows, width)
 
     def piece(x, index, size, axis):
         start = [0] * x.ndim
@@ -130,16 +127,15 @@
     count, bit = depth, 1
     block = half // depth
     total = total.reshape(count, block, total.shape[1])
-    while bit < NEAR:
+    while count > 1:
         mine = lax.shift_right_logical(me, bit.bit_length() - 1) & 1
         pairs = total.reshape(count // 2, 2, block, total.shape[2])
         away = piece(pairs, 1 - mine, 1, 1).squeeze(1).astype(BF16)
         kept = piece(pairs, mine, 1, 1).squeeze(1)
-        total = kept + with_partner(away, bit).astype(F32)
+        arrived = with_partner(away, bit)
+        total = kept + arrived.astype(F32)
         count, bit = count // 2, bit * 2
-    groups = [[x * depth + f * NEAR + k for f in range(count)] for x in range(2) for k in range(NEAR)]
-    parts = all_swap(total.astype(BF16), "dp", groups)
-    down_grad = jnp.sum(parts.astype(F32), axis=0)[None]
+    down_grad = total
 
     dact = lax.dot_general(cot, down_w, contract_last, preferred_element_type=F32)
     dgate = (dact * up_b * sig * (1.0 + gate_b * (1.0 - sig))).astype(BF16)

time: 157 us -> 154 us (0.981)
  the two profiles are of different devices: /device:TPU:4 before, /device:TPU:1 now
where the time goes in v1:
time: 154 us; the launch traced here: 153 us
  starting transfers between devices  81 us (53%)
  waiting for transfers between devices  41.7 us (27%)
  matrix products  14.5 us (9%)
  Pallas kernels  8.69 us (6%)
  local copies, waits for them, and re-layouts  4.55 us (3%)
  other arithmetic  1.85 us (1%)
    ppermute x7, starting transfers between devices, with_partner(): return lax.ppermute(x, 'dp', [(d, d ^ bit) for d in range(dp)])  42.3 us
    all_to_all x4, starting transfers between devices, exchange(): lax.all_to_all(x, 'ep', split_axis=0, concat_axis=0, tiled=True)  38.7 us
    ppermute x7, waiting for transfers between devices, with_partner(): return lax.ppermute(x, 'dp', [(d, d ^ bit) for d in range(dp)])  30.8 us
    all_to_all x4, waiting for transfers between devices, exchange(): lax.all_to_all(x, 'ep', split_axis=0, concat_axis=0, tiled=True)  10.9 us
    pallas_call x2, Pallas kernels, select(): pl.pallas_call(functools.partial(select_kernel, scaled), out_shape=jax.Sh...  4.36 us
    pallas_call x2, Pallas kernels, combine(): pl.pallas_call(functools.partial(combine_kernel, weighted), out_shape=jax...  4.34 us
    dot_general x1, matrix products, on_device(): row_a = jnp.dot(act_a, down_w, preferred_element_type=F32).astype(BF16)  3.22 us
  transfers between devices with their start and end apart: 11, of which 6 were waited for; matrix products, arithmetic and copies ran while one was open for 11% of the time, Pallas kernels for 4%

profile of v1, /device:TPU:1, one launch (start us, length us, event | category | flops | bytes accessed | tf_op | source)
XLA Modules:
  0.0 153.2 jit_solution(1231494207632632437)
XLA Ops:
  0.7 2.3 %select_scaled.1 = bf16[128,2048]{1,0:T(8,128)(2,1)} custom-call(s32[8,16]{1,0:T(8,128)} %bitcast.97, f32[8,16]{1,0:T(8,128)} %bitcast.99, bf16[16,2048]{1,0:T(8,128)(2,1)} %x_ref.3), custom_call_target="tpu_custom_call" | custom-call | flops 8388608 | bytes 1048576 | tf_op jit(solution)/shard_map/select_scaled/pallas_call | solution.py:48
  2.9 18.1 %all-to-all-start.2 = ((bf16[16,8,2048]{2,1,0:T(8,128)(2,1)}), bf16[16,8,2048]{2,1,0:T(8,128)(2,1)}, u32[]{:S(2)}, u32[]{:S(2)}) async-start(bf16[16,8,2048]{2,1,0:T(8,128)(2,1)} %bitcast.88), calls=%async_computation.2 | async-start | bytes 1048576 | tf_op jit(solution)/shard_map/all_to_all | solution.py:101
  21.0 2.1 %select_plain.1 = bf16[128,2048]{1,0:T(8,128)(2,1)} custom-call(s32[8,16]{1,0:T(8,128)} %bitcast.93, f32[8,16]{1,0:T(8,128)} %bitcast.95, bf16[16,2048]{1,0:T(8,128)(2,1)} %x_ref.2), custom_call_target="tpu_custom_call" | custom-call | flops 8388608 | bytes 1048576 | tf_op jit(solution)/shard_map/select_plain/pallas_call | solution.py:48
  23.1 9.3 %all-to-all-done.2 = bf16[16,8,2048]{2,1,0:T(8,128)(2,1)} async-done(((bf16[16,8,2048]{2,1,0:T(8,128)(2,1)}), bf16[16,8,2048]{2,1,0:T(8,128)(2,1)}, u32[]{:S(2)}, u32[]{:S(2)}) %all-to-all-start.2) | async-done | bytes 524320 | tf_op jit(solution)/shard_map/all_to_all | solution.py:101
  32.4 5.2 %all-to-all-start = ((bf16[16,8,2048]{2,1,0:T(8,128)(2,1)}), bf16[16,8,2048]{2,1,0:T(8,128)(2,1)}, u32[]{:S(2)}, u32[]{:S(2)}) async-start(bf16[16,8,2048]{2,1,0:T(8,128)(2,1)} %bitcast.86), calls=%async_computation | async-start | bytes 1048576 | tf_op jit(solution)/shard_map/all_to_all | solution.py:101
  37.6 1.5 %fusion.13 = f32[128,384]{1,0:T(8,128)S(1)} fusion(bf16[1,2048,384]{2,1,0:T(8,128)(2,1)S(1)} %copy-done.1, bf16[1,128,2048]{2,1,0:T(8,128)(2,1)} %param.16), kind=kOutput, calls=%fused_computation.15 | convolution fusion | flops 201326592 | bytes 2293760 | tf_op jit(solution)/shard_map/dot_general | solution.py:115
  39.2 1.2 multiply_convert_fusion
  40.4 1.9 %collective-permute-start.1 = (bf16[128,384]{1,0:T(8,128)(2,1)}, bf16[128,384]{1,0:T(8,128)(2,1)}, u32[]{:S(2)}, u32[]{:S(2)}) collective-permute-start(bf16[128,384]{1,0:T(8,128)(2,1)} %get-tuple-element.3), channel_id=1, source_target_pairs={{0,32},{1,33},{2,34},{3,35},{4,36},{5,37},{6,38},{7,39},{8,40},{9,... | collective-permute-start | bytes 294920 | tf_op jit(solution)/shard_map/ppermute | solution.py:110
  42.3 1.7 %constant_dynamic-slice_fusion = bf16[128,1024]{1,0:T(8,128)(2,1)} fusion(bf16[128,2048]{1,0:T(8,128)(2,1)} %bitcast.12, s32[]{:T(128)S(6)} %mul.48), kind=kLoop, calls=%fused_computation.54 | loop fusion | bytes 524292 | tf_op jit(solution)/shard_map/dynamic_slice | solution.py:107
  44.0 3.4 %collective-permute-start = (bf16[128,1024]{1,0:T(8,128)(2,1)}, bf16[128,1024]{1,0:T(8,128)(2,1)}, u32[]{:S(2)}, u32[]{:S(2)}) collective-permute-start(bf16[128,1024]{1,0:T(8,128)(2,1)} %constant_dynamic-slice_fusion), channel_id=1, source_target_pairs={{0,32},{1,33},{2,34},{3,35},{4,36},{5,37},{6,38},{7,39},{8,40},{9,... | collective-permute-start | bytes 786440 | tf_op jit(solution)/shard_map/ppermute | solution.py:110
  47.3 1.6 %all-to-all-done = bf16[16,8,2048]{2,1,0:T(8,128)(2,1)} async-done(((bf16[16,8,2048]{2,1,0:T(8,128)(2,1)}), bf16[16,8,2048]{2,1,0:T(8,128)(2,1)}, u32[]{:S(2)}, u32[]{:S(2)}) %all-to-all-start) | async-done | bytes 524320 | tf_op jit(solution)/shard_map/all_to_all | solution.py:101
  49.0 1.5 fusion.15
  50.4 1.4 fusion.31
  51.8 1.9 %collective-permute-done = bf16[128,1024]{1,0:T(8,128)(2,1)} collective-permute-done((bf16[128,1024]{1,0:T(8,128)(2,1)}, bf16[128,1024]{1,0:T(8,128)(2,1)}, u32[]{:S(2)}, u32[]{:S(2)}) %collective-permute-start) | collective-permute-done | bytes 262176 | tf_op jit(solution)/shard_map/ppermute | solution.py:110
  53.8 1.4 convolution_add_fusion.1
  55.1 1.2 copy-done.2
  57.1 1.9 %collective-permute-start.2 = (bf16[16,32,384]{2,1,0:T(8,128)(2,1)}, bf16[16,32,384]{2,1,0:T(8,128)(2,1)}, u32[]{:S(2)}, u32[]{:S(2)}) collective-permute-start(bf16[16,32,384]{2,1,0:T(8,128)(2,1)} %fusion.30), channel_id=1, source_target_pairs={{0,1},{1,0},{2,3},{3,2},{4,5},{5,4},{6,7},{7,6},{8,9},{9,8},{10,11... | collective-permute-start | bytes 1179656 | tf_op jit(solution)/shard_map/ppermute | solution.py:110
  59.0 3.2 %fusion.1 = bf16[16,8,2048]{2,1,0:T(8,128)(2,1)} fusion(bf16[1,384,2048]{2,1,0:T(8,128)(2,1)} %param.19, bf16[1,2048,384]{2,1,0:T(8,128)(2,1)S(1)} %copy-done, bf16[16,8,2048]{2,1,0:T(8,128)(2,1)} %all-to-all-done, f32[128,384]{1,0:T(8,128)S(1)} %fusion.15), kind=kOutput, calls=%fused_computation.3 | convolution fusion | flops 403210240 | bytes 4390912 | tf_op jit(solution)/shard_map/dot_general | solution.py:150
  62.2 8.1 %all-to-all-start.1 = ((bf16[16,8,2048]{2,1,0:T(8,128)(2,1)}), bf16[16,8,2048]{2,1,0:T(8,128)(2,1)}, u32[]{:S(2)}, u32[]{:S(2)}) async-start(bf16[16,8,2048]{2,1,0:T(8,128)(2,1)} %fusion.1), calls=%async_computation.1 | async-start | bytes 1048576 | tf_op jit(solution)/shard_map/all_to_all | solution.py:101
  70.3 2.3 %fusion.3 = f32[128,384]{1,0:T(8,128)S(1)} fusion(bf16[1,384,2048]{2,1,0:T(8,128)(2,1)} %param.19, bf16[16,8,2048]{2,1,0:T(8,128)(2,1)} %all-to-all-done.2), kind=kOutput, calls=%fused_computation.5 | convolution fusion | flops 201326592 | bytes 2293760 | tf_op jit(solution)/shard_map/dot_general | solution.py:140
  72.6 1.2 bitcast_add_fusion
  73.8 1.9 %collective-permute-start.3 = (bf16[8,32,384]{2,1,0:T(8,128)(2,1)S(1)}, bf16[8,32,384]{2,1,0:T(8,128)(2,1)S(1)}, u32[]{:S(2)}, u32[]{:S(2)}) collective-permute-start(bf16[8,32,384]{2,1,0:T(8,128)(2,1)S(1)} %fusion.33), channel_id=1, source_target_pairs={{0,2},{1,3},{2,0},{3,1},{4,6},{5,7},{6,4},{7,5},{8,10},{9,11},{10,... | collective-permute-start | bytes 589832 | tf_op jit(solution)/shard_map/ppermute | solution.py:110
  76.4 10.7 %collective-permute-done.3 = bf16[8,32,384]{2,1,0:T(8,128)(2,1)S(1)} collective-permute-done((bf16[8,32,384]{2,1,0:T(8,128)(2,1)S(1)}, bf16[8,32,384]{2,1,0:T(8,128)(2,1)S(1)}, u32[]{:S(2)}, u32[]{:S(2)}) %collective-permute-start.3) | collective-permute-done | bytes 196640 | tf_op jit(solution)/shard_map/ppermute | solution.py:110
  87.2 2.7 %collective-permute-start.4 = (bf16[4,32,384]{2,1,0:T(8,128)(2,1)S(1)}, bf16[4,32,384]{2,1,0:T(8,128)(2,1)S(1)}, u32[]{:S(2)}, u32[]{:S(2)}) collective-permute-start(bf16[4,32,384]{2,1,0:T(8,128)(2,1)S(1)} %fusion.39), channel_id=1, source_target_pairs={{0,4},{1,5},{2,6},{3,7},{4,0},{5,1},{6,2},{7,3},{8,12},{9,13},{10,... | collective-permute-start | bytes 294920 | tf_op jit(solution)/shard_map/ppermute | solution.py:110
  89.9 1.4 fusion.2
  91.3 11.1 %collective-permute-done.4 = bf16[4,32,384]{2,1,0:T(8,128)(2,1)S(1)} collective-permute-done((bf16[4,32,384]{2,1,0:T(8,128)(2,1)S(1)}, bf16[4,32,384]{2,1,0:T(8,128)(2,1)S(1)}, u32[]{:S(2)}, u32[]{:S(2)}) %collective-permute-start.4) | collective-permute-done | bytes 98336 | tf_op jit(solution)/shard_map/ppermute | solution.py:110
  102.5 7.3 %all-to-all-start.3 = ((bf16[16,8,2048]{2,1,0:T(8,128)(2,1)}), bf16[16,8,2048]{2,1,0:T(8,128)(2,1)S(1)}, u32[]{:S(2)}, u32[]{:S(2)}) async-start(bf16[16,8,2048]{2,1,0:T(8,128)(2,1)} %fusion.2), calls=%async_computation.3 | async-start | bytes 1048576 | tf_op jit(solution)/shard_map/all_to_all | solution.py:101
  109.8 10.9 %collective-permute-start.5 = (bf16[2,32,384]{2,1,0:T(8,128)(2,1)S(1)}, bf16[2,32,384]{2,1,0:T(8,128)(2,1)S(1)}, u32[]{:S(2)}, u32[]{:S(2)}) collective-permute-start(bf16[2,32,384]{2,1,0:T(8,128)(2,1)S(1)} %fusion.43), channel_id=1, source_target_pairs={{0,8},{1,9},{2,10},{3,11},{4,12},{5,13},{6,14},{7,15},{8,0},{9,1},... | collective-permute-start | bytes 147464 | tf_op jit(solution)/shard_map/ppermute | solution.py:110
  120.7 7.0 %collective-permute-done.5 = bf16[2,32,384]{2,1,0:T(8,128)(2,1)S(1)} collective-permute-done((bf16[2,32,384]{2,1,0:T(8,128)(2,1)S(1)}, bf16[2,32,384]{2,1,0:T(8,128)(2,1)S(1)}, u32[]{:S(2)}, u32[]{:S(2)}) %collective-permute-start.5) | collective-permute-done | bytes 49184 | tf_op jit(solution)/shard_map/ppermute | solution.py:110
  127.8 19.6 %collective-permute-start.6 = (bf16[1,32,384]{2,1,0:T(8,128)(2,1)S(1)}, bf16[1,32,384]{2,1,0:T(8,128)(2,1)S(1)}, u32[]{:S(2)}, u32[]{:S(2)}) collective-permute-start(bf16[1,32,384]{2,1,0:T(8,128)(2,1)S(1)} %dynamic-slice_convert_fusion.3), channel_id=1, source_target_pairs={{0,16},{1,17},{2,18},{3,19},{4,20},{5,21},{6,22},{7,23},{8,24},{9,... | collective-permute-start | bytes 73736 | tf_op jit(solution)/shard_map/ppermute | solution.py:110
  147.4 2.2 %combine_weighted.1 = bf16[16,2048]{1,0:T(8,128)(2,1)} custom-call(s32[8,16]{1,0:T(8,128)} %bitcast.94, f32[8,16]{1,0:T(8,128)} %bitcast.96, bf16[128,2048]{1,0:T(8,128)(2,1)} %bitcast.8.rows_ref), custom_call_target="tpu_custom_call" | custom-call | flops 10000000 | bytes 524288 | tf_op jit(solution)/shard_map/combine_weighted/pallas_call | solution.py:78
  150.5 2.1 %combine_plain.1 = bf16[16,2048]{1,0:T(8,128)(2,1)} custom-call(s32[8,16]{1,0:T(8,128)} %bitcast.98, f32[8,16]{1,0:T(8,128)} %bitcast.100, bf16[128,2048]{1,0:T(8,128)(2,1)} %bitcast.87), custom_call_target="tpu_custom_call" | custom-call | flops 10000000 | bytes 524288 | tf_op jit(solution)/shard_map/combine_plain/pallas_call | solution.py:78
  (28 shorter events, 3.1 us)
Async XLA Ops:
  0.6 38.5 %copy-start = (bf16[1,2048,384]{2,1,0:T(8,128)(2,1)S(1)}, bf16[1,2048,384]{2,1,0:T(8,128)(2,1)}, u32[]{:S(2)}) copy-start(bf16[1,2048,384]{2,1,0:T(8,128)(2,1)} %param.18) | copy-start | bytes 4718596
  0.6 37.0 %copy-start.1 = (bf16[1,2048,384]{2,1,0:T(8,128)(2,1)S(1)}, bf16[1,2048,384]{2,1,0:T(8,128)(2,1)}, u32[]{:S(2)}) copy-start(bf16[1,2048,384]{2,1,0:T(8,128)(2,1)} %param.17) | copy-start | bytes 4718596
  2.9 29.5 %all-to-all-start.2 = ((bf16[16,8,2048]{2,1,0:T(8,128)(2,1)}), bf16[16,8,2048]{2,1,0:T(8,128)(2,1)}, u32[]{:S(2)}, u32[]{:S(2)}) async-start(bf16[16,8,2048]{2,1,0:T(8,128)(2,1)} %bitcast.88), calls=%async_computation.2 | async-start | bytes 1048576 | tf_op jit(solution)/shard_map/all_to_all | solution.py:101
  32.4 16.6 %all-to-all-start = ((bf16[16,8,2048]{2,1,0:T(8,128)(2,1)}), bf16[16,8,2048]{2,1,0:T(8,128)(2,1)}, u32[]{:S(2)}, u32[]{:S(2)}) async-start(bf16[16,8,2048]{2,1,0:T(8,128)(2,1)} %bitcast.86), calls=%async_computation | async-start | bytes 1048576 | tf_op jit(solution)/shard_map/all_to_all | solution.py:101
  37.6 1.6 %copy-start.5 = (bf16[1,128,2048]{2,1,0:T(8,128)(2,1)S(1)}, bf16[1,128,2048]{2,1,0:T(8,128)(2,1)}, u32[]{:S(2)}) copy-start(bf16[1,128,2048]{2,1,0:T(8,128)(2,1)} %param.16) | copy-start | bytes 1572868
  40.4 11.4 %collective-permute-start.1 = (bf16[128,384]{1,0:T(8,128)(2,1)}, bf16[128,384]{1,0:T(8,128)(2,1)}, u32[]{:S(2)}, u32[]{:S(2)}) collective-permute-start(bf16[128,384]{1,0:T(8,128)(2,1)} %get-tuple-element.3), channel_id=1, source_target_pairs={{0,32},{1,33},{2,34},{3,35},{4,36},{5,37},{6,38},{7,39},{8,40},{9,... | collective-permute-start | bytes 294920 | tf_op jit(solution)/shard_map/ppermute | solution.py:110
  44.0 9.8 %collective-permute-start = (bf16[128,1024]{1,0:T(8,128)(2,1)}, bf16[128,1024]{1,0:T(8,128)(2,1)}, u32[]{:S(2)}, u32[]{:S(2)}) collective-permute-start(bf16[128,1024]{1,0:T(8,128)(2,1)} %constant_dynamic-slice_fusion), channel_id=1, source_target_pairs={{0,32},{1,33},{2,34},{3,35},{4,36},{5,37},{6,38},{7,39},{8,40},{9,... | collective-permute-start | bytes 786440 | tf_op jit(solution)/shard_map/ppermute | solution.py:110
  55.1 1.2 copy-start.2
  57.1 15.5 %collective-permute-start.2 = (bf16[16,32,384]{2,1,0:T(8,128)(2,1)}, bf16[16,32,384]{2,1,0:T(8,128)(2,1)}, u32[]{:S(2)}, u32[]{:S(2)}) collective-permute-start(bf16[16,32,384]{2,1,0:T(8,128)(2,1)} %fusion.30), channel_id=1, source_target_pairs={{0,1},{1,0},{2,3},{3,2},{4,5},{5,4},{6,7},{7,6},{8,9},{9,8},{10,11... | collective-permute-start | bytes 1179656 | tf_op jit(solution)/shard_map/ppermute | solution.py:110
  62.2 40.2 %all-to-all-start.1 = ((bf16[16,8,2048]{2,1,0:T(8,128)(2,1)}), bf16[16,8,2048]{2,1,0:T(8,128)(2,1)}, u32[]{:S(2)}, u32[]{:S(2)}) async-start(bf16[16,8,2048]{2,1,0:T(8,128)(2,1)} %fusion.1), calls=%async_computation.1 | async-start | bytes 1048576 | tf_op jit(solution)/shard_map/all_to_all | solution.py:101
  70.3 2.3 %copy-start.3 = (f32[1024,384]{1,0:T(8,128)S(1)}, f32[1024,384]{1,0:T(8,128)}, u32[]{:S(2)}) copy-start(f32[1024,384]{1,0:T(8,128)} %copy-done.2) | copy-start | bytes 4718596
  72.6 3.2 %copy-start.6 = (f32[128,384]{1,0:T(8,128)S(1)}, f32[128,384]{1,0:T(8,128)}, u32[]{:S(2)}) copy-start(f32[128,384]{1,0:T(8,128)} %get-tuple-element.4) | copy-start | bytes 589828
  73.8 13.3 %collective-permute-start.3 = (bf16[8,32,384]{2,1,0:T(8,128)(2,1)S(1)}, bf16[8,32,384]{2,1,0:T(8,128)(2,1)S(1)}, u32[]{:S(2)}, u32[]{:S(2)}) collective-permute-start(bf16[8,32,384]{2,1,0:T(8,128)(2,1)S(1)} %fusion.33), channel_id=1, source_target_pairs={{0,2},{1,3},{2,0},{3,1},{4,6},{5,7},{6,4},{7,5},{8,10},{9,11},{10,... | collective-permute-start | bytes 589832 | tf_op jit(solution)/shard_map/ppermute | solution.py:110
  87.2 15.2 %collective-permute-start.4 = (bf16[4,32,384]{2,1,0:T(8,128)(2,1)S(1)}, bf16[4,32,384]{2,1,0:T(8,128)(2,1)S(1)}, u32[]{:S(2)}, u32[]{:S(2)}) collective-permute-start(bf16[4,32,384]{2,1,0:T(8,128)(2,1)S(1)} %fusion.39), channel_id=1, source_target_pairs={{0,4},{1,5},{2,6},{3,7},{4,0},{5,1},{6,2},{7,3},{8,12},{9,13},{10,... | collective-permute-start | bytes 294920 | tf_op jit(solution)/shard_map/ppermute | solution.py:110
  102.5 47.2 %all-to-all-start.3 = ((bf16[16,8,2048]{2,1,0:T(8,128)(2,1)}), bf16[16,8,2048]{2,1,0:T(8,128)(2,1)S(1)}, u32[]{:S(2)}, u32[]{:S(2)}) async-start(bf16[16,8,2048]{2,1,0:T(8,128)(2,1)} %fusion.2), calls=%async_computation.3 | async-start | bytes 1048576 | tf_op jit(solution)/shard_map/all_to_all | solution.py:101
  109.8 18.0 %collective-permute-start.5 = (bf16[2,32,384]{2,1,0:T(8,128)(2,1)S(1)}, bf16[2,32,384]{2,1,0:T(8,128)(2,1)S(1)}, u32[]{:S(2)}, u32[]{:S(2)}) collective-permute-start(bf16[2,32,384]{2,1,0:T(8,128)(2,1)S(1)} %fusion.43), channel_id=1, source_target_pairs={{0,8},{1,9},{2,10},{3,11},{4,12},{5,13},{6,14},{7,15},{8,0},{9,1},... | collective-permute-start | bytes 147464 | tf_op jit(solution)/shard_map/ppermute | solution.py:110
  127.8 24.8 %collective-permute-start.6 = (bf16[1,32,384]{2,1,0:T(8,128)(2,1)S(1)}, bf16[1,32,384]{2,1,0:T(8,128)(2,1)S(1)}, u32[]{:S(2)}, u32[]{:S(2)}) collective-permute-start(bf16[1,32,384]{2,1,0:T(8,128)(2,1)S(1)} %dynamic-slice_convert_fusion.3), channel_id=1, source_target_pairs={{0,16},{1,17},{2,18},{3,19},{4,20},{5,21},{6,22},{7,23},{8,24},{9,... | collective-permute-start | bytes 73736 | tf_op jit(solution)/shard_map/ppermute | solution.py:110
  149.7 0.8 copy-start.4

commit v2 on v1

--- a/solution.py
+++ b/solution.py
@@ -6,6 +6,7 @@
 
 EXPERTS = 16
 SLOTS = 8
+FAR = 4
 BF16, F32 = jnp.bfloat16, jnp.float32
 
 
@@ -126,16 +127,31 @@
 
     count, bit = depth, 1
     block = half // depth
-    total = total.reshape(count, block, total.shape[1])
-    while count > 1:
+    kept, arrived = total.reshape(count, block, total.shape[1]), None
+
+    def share(index, group):
+        def part(x):
+            x = x.reshape((x.shape[0] // group, group) + x.shape[1:])
+            return piece(x, index, 1, 1).squeeze(1)
+
+        mine = part(kept)
+        return mine if arrived is None else mine + part(arrived).astype(F32)
+
+    while count > FAR:
         mine = lax.shift_right_logical(me, bit.bit_length() - 1) & 1
-        pairs = total.reshape(count // 2, 2, block, total.shape[2])
-        away = piece(pairs, 1 - mine, 1, 1).squeeze(1).astype(BF16)
-        kept = piece(pairs, mine, 1, 1).squeeze(1)
-        arrived = with_partner(away, bit)
-        total = kept + arrived.astype(F32)
+        away = share(1 - mine, 2).astype(BF16)
+        next_kept = share(mine, 2)
+        kept, arrived = next_kept, with_partner(away, bit)
         count, bit = count // 2, bit * 2
-    down_grad = total
+
+    mine = lax.shift_right_logical(me, bit.bit_length() - 1) & (FAR - 1)
+    down_grad, shares = None, []
+    for step in (2, 1, 3):
+        away = share(mine ^ step, FAR).astype(BF16)
+        shares.append(with_partner(away, step * bit))
+    down_grad = share(mine, FAR)
+    for part in shares:
+        down_grad = down_grad + part.astype(F32)
 
     dact = lax.dot_general(cot, down_w, contract_last, preferred_element_type=F32)
     dgate = (dact * up_b * sig * (1.0 + gate_b * (1.0 - sig))).astype(BF16)

time: 154 us -> 158 us (1.026)
  the two profiles are of different devices: /device:TPU:1 before, /device:TPU:4 now
where the time goes in v2:
time: 158 us; the launch traced here: 157 us
  starting transfers between devices  79 us (50%)
  waiting for transfers between devices  51.1 us (32%)
  matrix products  14.3 us (9%)
  Pallas kernels  8.7 us (6%)
  local copies, waits for them, and re-layouts  1.92 us (1%)
    ppermute x8, waiting for transfers between devices, with_partner(): return lax.ppermute(x, 'dp', [(d, d ^ bit) for d in range(dp)])  42.9 us
    ppermute x8, starting transfers between devices, with_partner(): return lax.ppermute(x, 'dp', [(d, d ^ bit) for d in range(dp)])  40.6 us
    all_to_all x4, starting transfers between devices, exchange(): lax.all_to_all(x, 'ep', split_axis=0, concat_axis=0, tiled=True)  38.5 us
    all_to_all x4, waiting for transfers between devices, exchange(): lax.all_to_all(x, 'ep', split_axis=0, concat_axis=0, tiled=True)  8.17 us
    pallas_call x2, Pallas kernels, select(): pl.pallas_call(functools.partial(select_kernel, scaled), out_shape=jax.Sh...  4.37 us
    pallas_call x2, Pallas kernels, combine(): pl.pallas_call(functools.partial(combine_kernel, weighted), out_shape=jax...  4.34 us
    dot_general x1, matrix products, on_device(): row_a = jnp.dot(act_a, down_w, preferred_element_type=F32).astype(BF16)  3.22 us
  transfers between devices with their start and end apart: 12, of which 7 were waited for; matrix products, arithmetic and copies ran while one was open for 10% of the time, Pallas kernels for 4%

profile of v2, /device:TPU:4, one launch (start us, length us, event | category | flops | bytes accessed | tf_op | source)
XLA Modules:
  0.0 156.7 jit_solution(10633354411373758073)
XLA Ops:
  0.7 2.3 %select_plain.1 = bf16[128,2048]{1,0:T(8,128)(2,1)} custom-call(s32[8,16]{1,0:T(8,128)} %bitcast.104, f32[8,16]{1,0:T(8,128)} %bitcast.106, bf16[16,2048]{1,0:T(8,128)(2,1)} %x_ref.2), custom_call_target="tpu_custom_call" | custom-call | flops 8388608 | bytes 1048576 | tf_op jit(solution)/shard_map/select_plain/pallas_call | solution.py:49
  2.9 17.2 %all-to-all-start = ((bf16[16,8,2048]{2,1,0:T(8,128)(2,1)}), bf16[16,8,2048]{2,1,0:T(8,128)(2,1)}, u32[]{:S(2)}, u32[]{:S(2)}) async-start(bf16[16,8,2048]{2,1,0:T(8,128)(2,1)} %bitcast.99), calls=%async_computation | async-start | bytes 1048576 | tf_op jit(solution)/shard_map/all_to_all | solution.py:102
  20.1 1.5 fusion.13
  21.6 1.2 multiply_convert_fusion
  22.8 1.9 %collective-permute-start.1 = (bf16[128,384]{1,0:T(8,128)(2,1)}, bf16[128,384]{1,0:T(8,128)(2,1)}, u32[]{:S(2)}, u32[]{:S(2)}) collective-permute-start(bf16[128,384]{1,0:T(8,128)(2,1)} %get-tuple-element.10), channel_id=1, source_target_pairs={{0,32},{1,33},{2,34},{3,35},{4,36},{5,37},{6,38},{7,39},{8,40},{9,... | collective-permute-start | bytes 294920 | tf_op jit(solution)/shard_map/ppermute | solution.py:111
  24.8 2.1 %select_scaled.1 = bf16[128,2048]{1,0:T(8,128)(2,1)} custom-call(s32[8,16]{1,0:T(8,128)} %bitcast.108, f32[8,16]{1,0:T(8,128)} %bitcast.110, bf16[16,2048]{1,0:T(8,128)(2,1)} %x_ref.3), custom_call_target="tpu_custom_call" | custom-call | flops 8388608 | bytes 1048576 | tf_op jit(solution)/shard_map/select_scaled/pallas_call | solution.py:49
  26.9 3.3 %all-to-all-done = bf16[16,8,2048]{2,1,0:T(8,128)(2,1)} async-done(((bf16[16,8,2048]{2,1,0:T(8,128)(2,1)}), bf16[16,8,2048]{2,1,0:T(8,128)(2,1)}, u32[]{:S(2)}, u32[]{:S(2)}) %all-to-all-start) | async-done | bytes 524320 | tf_op jit(solution)/shard_map/all_to_all | solution.py:102
  30.2 7.0 %all-to-all-start.2 = ((bf16[16,8,2048]{2,1,0:T(8,128)(2,1)}), bf16[16,8,2048]{2,1,0:T(8,128)(2,1)}, u32[]{:S(2)}, u32[]{:S(2)}) async-start(bf16[16,8,2048]{2,1,0:T(8,128)(2,1)} %bitcast.100), calls=%async_computation.2 | async-start | bytes 1048576 | tf_op jit(solution)/shard_map/all_to_all | solution.py:102
  37.2 1.5 fusion.15
  38.7 3.2 %fusion.1 = bf16[16,8,2048]{2,1,0:T(8,128)(2,1)} fusion(bf16[1,384,2048]{2,1,0:T(8,128)(2,1)} %param.19, bf16[1,2048,384]{2,1,0:T(8,128)(2,1)S(1)} %copy-done, bf16[16,8,2048]{2,1,0:T(8,128)(2,1)} %all-to-all-done, f32[128,384]{1,0:T(8,128)S(1)} %fusion.15), kind=kOutput, calls=%fused_computation.3 | convolution fusion | flops 403210240 | bytes 4390912 | tf_op jit(solution)/shard_map/dot_general | solution.py:166
  41.9 4.9 %all-to-all-done.2 = bf16[16,8,2048]{2,1,0:T(8,128)(2,1)} async-done(((bf16[16,8,2048]{2,1,0:T(8,128)(2,1)}), bf16[16,8,2048]{2,1,0:T(8,128)(2,1)}, u32[]{:S(2)}, u32[]{:S(2)}) %all-to-all-start.2) | async-done | bytes 524320 | tf_op jit(solution)/shard_map/all_to_all | solution.py:102
  46.8 7.0 %all-to-all-start.1 = ((bf16[16,8,2048]{2,1,0:T(8,128)(2,1)}), bf16[16,8,2048]{2,1,0:T(8,128)(2,1)}, u32[]{:S(2)}, u32[]{:S(2)}) async-start(bf16[16,8,2048]{2,1,0:T(8,128)(2,1)} %fusion.1), calls=%async_computation.1 | async-start | bytes 1048576 | tf_op jit(solution)/shard_map/all_to_all | solution.py:102
  53.8 1.0 constant_dynamic-slice_fusion.1
  54.8 1.9 %collective-permute-start = (bf16[128,1024]{1,0:T(8,128)(2,1)S(1)}, bf16[128,1024]{1,0:T(8,128)(2,1)S(1)}, u32[]{:S(2)}, u32[]{:S(2)}) collective-permute-start(bf16[128,1024]{1,0:T(8,128)(2,1)S(1)} %constant_dynamic-slice_fusion.1), channel_id=1, source_target_pairs={{0,32},{1,33},{2,34},{3,35},{4,36},{5,37},{6,38},{7,39},{8,40},{9,... | collective-permute-start | bytes 786440 | tf_op jit(solution)/shard_map/ppermute | solution.py:111
  56.7 2.2 %fusion.3 = f32[128,384]{1,0:T(8,128)S(1)} fusion(bf16[1,384,2048]{2,1,0:T(8,128)(2,1)} %param.19, bf16[16,8,2048]{2,1,0:T(8,128)(2,1)} %all-to-all-done.2), kind=kOutput, calls=%fused_computation.5 | convolution fusion | flops 201326592 | bytes 2293760 | tf_op jit(solution)/shard_map/dot_general | solution.py:156
  58.9 1.4 fusion.31
  60.3 5.5 %collective-permute-done = bf16[128,1024]{1,0:T(8,128)(2,1)S(1)} collective-permute-done((bf16[128,1024]{1,0:T(8,128)(2,1)S(1)}, bf16[128,1024]{1,0:T(8,128)(2,1)S(1)}, u32[]{:S(2)}, u32[]{:S(2)}) %collective-permute-start) | collective-permute-done | bytes 262176 | tf_op jit(solution)/shard_map/ppermute | solution.py:111
  65.8 1.3 convolution_add_fusion.1
  67.1 1.9 %collective-permute-start.2 = (bf16[16,32,384]{2,1,0:T(8,128)(2,1)S(1)}, bf16[16,32,384]{2,1,0:T(8,128)(2,1)S(1)}, u32[]{:S(2)}, u32[]{:S(2)}) collective-permute-start(bf16[16,32,384]{2,1,0:T(8,128)(2,1)S(1)} %fusion.30), channel_id=1, source_target_pairs={{0,1},{1,0},{2,3},{3,2},{4,5},{5,4},{6,7},{7,6},{8,9},{9,8},{10,11... | collective-permute-start | bytes 1179656 | tf_op jit(solution)/shard_map/ppermute | solution.py:111
  69.8 9.8 %collective-permute-done.2 = bf16[16,32,384]{2,1,0:T(8,128)(2,1)S(1)} collective-permute-done((bf16[16,32,384]{2,1,0:T(8,128)(2,1)S(1)}, bf16[16,32,384]{2,1,0:T(8,128)(2,1)S(1)}, u32[]{:S(2)}, u32[]{:S(2)}) %collective-permute-start.2) | collective-permute-done | bytes 393248 | tf_op jit(solution)/shard_map/ppermute | solution.py:111
  79.7 1.9 %collective-permute-start.3 = (bf16[8,32,384]{2,1,0:T(8,128)(2,1)S(1)}, bf16[8,32,384]{2,1,0:T(8,128)(2,1)S(1)}, u32[]{:S(2)}, u32[]{:S(2)}) collective-permute-start(bf16[8,32,384]{2,1,0:T(8,128)(2,1)S(1)} %get-tuple-element.3), channel_id=1, source_target_pairs={{0,2},{1,3},{2,0},{3,1},{4,6},{5,7},{6,4},{7,5},{8,10},{9,11},{10,... | collective-permute-start | bytes 589832 | tf_op jit(solution)/shard_map/ppermute | solution.py:111
  81.6 1.4 fusion.2
  83.1 7.3 %all-to-all-start.3 = ((bf16[16,8,2048]{2,1,0:T(8,128)(2,1)}), bf16[16,8,2048]{2,1,0:T(8,128)(2,1)S(1)}, u32[]{:S(2)}, u32[]{:S(2)}) async-start(bf16[16,8,2048]{2,1,0:T(8,128)(2,1)} %fusion.2), calls=%async_computation.3 | async-start | bytes 1048576 | tf_op jit(solution)/shard_map/all_to_all | solution.py:102
  90.3 1.9 %collective-permute-done.3 = bf16[8,32,384]{2,1,0:T(8,128)(2,1)S(1)} collective-permute-done((bf16[8,32,384]{2,1,0:T(8,128)(2,1)S(1)}, bf16[8,32,384]{2,1,0:T(8,128)(2,1)S(1)}, u32[]{:S(2)}, u32[]{:S(2)}) %collective-permute-start.3) | collective-permute-done | bytes 196640 | tf_op jit(solution)/shard_map/ppermute | solution.py:111
  92.3 2.4 %collective-permute-start.4 = (bf16[4,32,384]{2,1,0:T(8,128)(2,1)S(1)}, bf16[4,32,384]{2,1,0:T(8,128)(2,1)S(1)}, u32[]{:S(2)}, u32[]{:S(2)}) collective-permute-start(bf16[4,32,384]{2,1,0:T(8,128)(2,1)S(1)} %get-tuple-element.5), channel_id=1, source_target_pairs={{0,4},{1,5},{2,6},{3,7},{4,0},{5,1},{6,2},{7,3},{8,12},{9,13},{10,... | collective-permute-start | bytes 294920 | tf_op jit(solution)/shard_map/ppermute | solution.py:111
  94.7 12.4 %collective-permute-done.4 = bf16[4,32,384]{2,1,0:T(8,128)(2,1)S(1)} collective-permute-done((bf16[4,32,384]{2,1,0:T(8,128)(2,1)S(1)}, bf16[4,32,384]{2,1,0:T(8,128)(2,1)S(1)}, u32[]{:S(2)}, u32[]{:S(2)}) %collective-permute-start.4) | collective-permute-done | bytes 98336 | tf_op jit(solution)/shard_map/ppermute | solution.py:111
  107.1 16.5 %collective-permute-start.7 = (bf16[1,32,384]{2,1,0:T(8,128)(2,1)S(1)}, bf16[1,32,384]{2,1,0:T(8,128)(2,1)S(1)}, u32[]{:S(2)}, u32[]{:S(2)}) collective-permute-start(bf16[1,32,384]{2,1,0:T(8,128)(2,1)S(1)} %get-tuple-element.8), channel_id=1, source_target_pairs={{0,24},{1,25},{2,26},{3,27},{4,28},{5,29},{6,30},{7,31},{8,16},{9,... | collective-permute-start | bytes 73736 | tf_op jit(solution)/shard_map/ppermute | solution.py:111
  123.5 8.5 %collective-permute-start.6 = (bf16[1,32,384]{2,1,0:T(8,128)(2,1)S(1)}, bf16[1,32,384]{2,1,0:T(8,128)(2,1)S(1)}, u32[]{:S(2)}, u32[]{:S(2)}) collective-permute-start(bf16[1,32,384]{2,1,0:T(8,128)(2,1)S(1)} %get-tuple-element.9), channel_id=1, source_target_pairs={{0,8},{1,9},{2,10},{3,11},{4,12},{5,13},{6,14},{7,15},{8,0},{9,1},... | collective-permute-start | bytes 73736 | tf_op jit(solution)/shard_map/ppermute | solution.py:111
  132.0 5.5 %collective-permute-start.5 = (bf16[1,32,384]{2,1,0:T(8,128)(2,1)S(1)}, bf16[1,32,384]{2,1,0:T(8,128)(2,1)S(1)}, u32[]{:S(2)}, u32[]{:S(2)}) collective-permute-start(bf16[1,32,384]{2,1,0:T(8,128)(2,1)S(1)} %get-tuple-element.7), channel_id=1, source_target_pairs={{0,16},{1,17},{2,18},{3,19},{4,20},{5,21},{6,22},{7,23},{8,24},{9,... | collective-permute-start | bytes 73736 | tf_op jit(solution)/shard_map/ppermute | solution.py:111
  137.6 2.2 %combine_weighted.1 = bf16[16,2048]{1,0:T(8,128)(2,1)} custom-call(s32[8,16]{1,0:T(8,128)} %bitcast.105, f32[8,16]{1,0:T(8,128)} %bitcast.107, bf16[128,2048]{1,0:T(8,128)(2,1)} %bitcast.8.rows_ref), custom_call_target="tpu_custom_call" | custom-call | flops 10000000 | bytes 524288 | tf_op jit(solution)/shard_map/combine_weighted/pallas_call | solution.py:79
  140.6 2.1 %combine_plain.1 = bf16[16,2048]{1,0:T(8,128)(2,1)} custom-call(s32[8,16]{1,0:T(8,128)} %bitcast.109, f32[8,16]{1,0:T(8,128)} %bitcast.111, bf16[128,2048]{1,0:T(8,128)(2,1)} %bitcast.98), custom_call_target="tpu_custom_call" | custom-call | flops 10000000 | bytes 524288 | tf_op jit(solution)/shard_map/combine_plain/pallas_call | solution.py:79
  142.7 13.4 %collective-permute-done.5 = bf16[1,32,384]{2,1,0:T(8,128)(2,1)S(1)} collective-permute-done((bf16[1,32,384]{2,1,0:T(8,128)(2,1)S(1)}, bf16[1,32,384]{2,1,0:T(8,128)(2,1)S(1)}, u32[]{:S(2)}, u32[]{:S(2)}) %collective-permute-start.5) | collective-permute-done | bytes 24608 | tf_op jit(solution)/shard_map/ppermute | solution.py:111
  (22 shorter events, 2.4 us)
Async XLA Ops:
  0.6 21.0 %copy-start = (bf16[1,2048,384]{2,1,0:T(8,128)(2,1)S(1)}, bf16[1,2048,384]{2,1,0:T(8,128)(2,1)}, u32[]{:S(2)}) copy-start(bf16[1,2048,384]{2,1,0:T(8,128)(2,1)} %param.18) | copy-start | bytes 4718596
  0.6 19.4 %copy-start.1 = (bf16[1,2048,384]{2,1,0:T(8,128)(2,1)S(1)}, bf16[1,2048,384]{2,1,0:T(8,128)(2,1)}, u32[]{:S(2)}) copy-start(bf16[1,2048,384]{2,1,0:T(8,128)(2,1)} %param.17) | copy-start | bytes 4718596
  2.9 27.3 %all-to-all-start = ((bf16[16,8,2048]{2,1,0:T(8,128)(2,1)}), bf16[16,8,2048]{2,1,0:T(8,128)(2,1)}, u32[]{:S(2)}, u32[]{:S(2)}) async-start(bf16[16,8,2048]{2,1,0:T(8,128)(2,1)} %bitcast.99), calls=%async_computation | async-start | bytes 1048576 | tf_op jit(solution)/shard_map/all_to_all | solution.py:102
  20.1 1.6 copy-start.3
  22.8 37.5 %collective-permute-start.1 = (bf16[128,384]{1,0:T(8,128)(2,1)}, bf16[128,384]{1,0:T(8,128)(2,1)}, u32[]{:S(2)}, u32[]{:S(2)}) collective-permute-start(bf16[128,384]{1,0:T(8,128)(2,1)} %get-tuple-element.10), channel_id=1, source_target_pairs={{0,32},{1,33},{2,34},{3,35},{4,36},{5,37},{6,38},{7,39},{8,40},{9,... | collective-permute-start | bytes 294920 | tf_op jit(solution)/shard_map/ppermute | solution.py:111
  30.2 16.6 %all-to-all-start.2 = ((bf16[16,8,2048]{2,1,0:T(8,128)(2,1)}), bf16[16,8,2048]{2,1,0:T(8,128)(2,1)}, u32[]{:S(2)}, u32[]{:S(2)}) async-start(bf16[16,8,2048]{2,1,0:T(8,128)(2,1)} %bitcast.100), calls=%async_computation.2 | async-start | bytes 1048576 | tf_op jit(solution)/shard_map/all_to_all | solution.py:102
  46.8 36.3 %all-to-all-start.1 = ((bf16[16,8,2048]{2,1,0:T(8,128)(2,1)}), bf16[16,8,2048]{2,1,0:T(8,128)(2,1)}, u32[]{:S(2)}, u32[]{:S(2)}) async-start(bf16[16,8,2048]{2,1,0:T(8,128)(2,1)} %fusion.1), calls=%async_computation.1 | async-start | bytes 1048576 | tf_op jit(solution)/shard_map/all_to_all | solution.py:102
  54.8 11.0 %collective-permute-start = (bf16[128,1024]{1,0:T(8,128)(2,1)S(1)}, bf16[128,1024]{1,0:T(8,128)(2,1)S(1)}, u32[]{:S(2)}, u32[]{:S(2)}) collective-permute-start(bf16[128,1024]{1,0:T(8,128)(2,1)S(1)} %constant_dynamic-slice_fusion.1), channel_id=1, source_target_pairs={{0,32},{1,33},{2,34},{3,35},{4,36},{5,37},{6,38},{7,39},{8,40},{9,... | collective-permute-start | bytes 786440 | tf_op jit(solution)/shard_map/ppermute | solution.py:111
  60.3 8.8 %copy-start.4 = (f32[128,384]{1,0:T(8,128)S(1)}, f32[128,384]{1,0:T(8,128)}, u32[]{:S(2)}) copy-start(f32[128,384]{1,0:T(8,128)} %get-tuple-element.11) | copy-start | bytes 589828
  67.1 12.5 %collective-permute-start.2 = (bf16[16,32,384]{2,1,0:T(8,128)(2,1)S(1)}, bf16[16,32,384]{2,1,0:T(8,128)(2,1)S(1)}, u32[]{:S(2)}, u32[]{:S(2)}) collective-permute-start(bf16[16,32,384]{2,1,0:T(8,128)(2,1)S(1)} %fusion.30), channel_id=1, source_target_pairs={{0,1},{1,0},{2,3},{3,2},{4,5},{5,4},{6,7},{7,6},{8,9},{9,8},{10,11... | collective-permute-start | bytes 1179656 | tf_op jit(solution)/shard_map/ppermute | solution.py:111
  79.7 12.5 %collective-permute-start.3 = (bf16[8,32,384]{2,1,0:T(8,128)(2,1)S(1)}, bf16[8,32,384]{2,1,0:T(8,128)(2,1)S(1)}, u32[]{:S(2)}, u32[]{:S(2)}) collective-permute-start(bf16[8,32,384]{2,1,0:T(8,128)(2,1)S(1)} %get-tuple-element.3), channel_id=1, source_target_pairs={{0,2},{1,3},{2,0},{3,1},{4,6},{5,7},{6,4},{7,5},{8,10},{9,11},{10,... | collective-permute-start | bytes 589832 | tf_op jit(solution)/shard_map/ppermute | solution.py:111
  83.1 56.8 %all-to-all-start.3 = ((bf16[16,8,2048]{2,1,0:T(8,128)(2,1)}), bf16[16,8,2048]{2,1,0:T(8,128)(2,1)S(1)}, u32[]{:S(2)}, u32[]{:S(2)}) async-start(bf16[16,8,2048]{2,1,0:T(8,128)(2,1)} %fusion.2), calls=%async_computation.3 | async-start | bytes 1048576 | tf_op jit(solution)/shard_map/all_to_all | solution.py:102
  92.3 14.8 %collective-permute-start.4 = (bf16[4,32,384]{2,1,0:T(8,128)(2,1)S(1)}, bf16[4,32,384]{2,1,0:T(8,128)(2,1)S(1)}, u32[]{:S(2)}, u32[]{:S(2)}) collective-permute-start(bf16[4,32,384]{2,1,0:T(8,128)(2,1)S(1)} %get-tuple-element.5), channel_id=1, source_target_pairs={{0,4},{1,5},{2,6},{3,7},{4,0},{5,1},{6,2},{7,3},{8,12},{9,13},{10,... | collective-permute-start | bytes 294920 | tf_op jit(solution)/shard_map/ppermute | solution.py:111
  107.1 35.7 %collective-permute-start.7 = (bf16[1,32,384]{2,1,0:T(8,128)(2,1)S(1)}, bf16[1,32,384]{2,1,0:T(8,128)(2,1)S(1)}, u32[]{:S(2)}, u32[]{:S(2)}) collective-permute-start(bf16[1,32,384]{2,1,0:T(8,128)(2,1)S(1)} %get-tuple-element.8), channel_id=1, source_target_pairs={{0,24},{1,25},{2,26},{3,27},{4,28},{5,29},{6,30},{7,31},{8,16},{9,... | collective-permute-start | bytes 73736 | tf_op jit(solution)/shard_map/ppermute | solution.py:111
  123.5 19.2 %collective-permute-start.6 = (bf16[1,32,384]{2,1,0:T(8,128)(2,1)S(1)}, bf16[1,32,384]{2,1,0:T(8,128)(2,1)S(1)}, u32[]{:S(2)}, u32[]{:S(2)}) collective-permute-start(bf16[1,32,384]{2,1,0:T(8,128)(2,1)S(1)} %get-tuple-element.9), channel_id=1, source_target_pairs={{0,8},{1,9},{2,10},{3,11},{4,12},{5,13},{6,14},{7,15},{8,0},{9,1},... | collective-permute-start | bytes 73736 | tf_op jit(solution)/shard_map/ppermute | solution.py:111
  132.0 24.0 %collective-permute-start.5 = (bf16[1,32,384]{2,1,0:T(8,128)(2,1)S(1)}, bf16[1,32,384]{2,1,0:T(8,128)(2,1)S(1)}, u32[]{:S(2)}, u32[]{:S(2)}) collective-permute-start(bf16[1,32,384]{2,1,0:T(8,128)(2,1)S(1)} %get-tuple-element.7), channel_id=1, source_target_pairs={{0,16},{1,17},{2,18},{3,19},{4,20},{5,21},{6,22},{7,23},{8,24},{9,... | collective-permute-start | bytes 73736 | tf_op jit(solution)/shard_map/ppermute | solution.py:111
  139.8 0.8 copy-start.2
